TPU v7x, 128 devices: a whole 4x4x4 slice. The times are simulated.
128 devices in a mesh: row: 8 (over y, core), col: 16 (over z, x).
Axes of the slice: x: 4, y: 4, z: 4, core: 2. Of those that a mesh axis runs over, the one named last changes fastest.
Arguments:
- wavefunction: bfloat16 [32, 16, 256, 256], P('row', 'col'), may hold values from -6 to 6
- env_left: bfloat16 [16, 32, 2, 256, 256], P('col', 'row'), may hold values from -0.25 to 0.25
- left_src: int32 [16, 32, 2], P('col', 'row'), may hold values from 0 to 3
- two_site: bfloat16 [16, 16, 16], P('col'), may hold values from -1.5 to 1.5
- env_right: bfloat16 [16, 32, 256, 256], P('col', 'row'), may hold values from -0.09375 to 0.09375
- right_loc: int32 [32, 16], P('row', 'col'), may hold values from 0 to 3
- left_size: int32 [32], P('row'), may hold values from 128 to 256
- right_size: int32 [32], P('row'), may hold values from 128 to 256
Outputs:
- applied: bfloat16 [32, 16, 256, 256], P('row', 'col')
All inputs are finite; a program needn't handle non-finite values.
Results may differ from a plain program's by a relative error of at most 0.018.
Values may be sent and summed in bfloat16 or wider, within the bound.
No kernel may reach another device: no remote copies, remote signals or barrier semaphores. Data moves between devices by JAX's collectives and lax.ppermute only.
A program may use at most 128 MiB of HBM per device.

v0:
```python
import jax
import jax.numpy as jnp
from jax import lax
from jax.sharding import PartitionSpec as P


def per_device(
    wavefunction, env_left, left_src, two_site, env_right, right_loc, left_size, right_size
):
    whole, whole_loc = (
        lax.all_gather(wavefunction, "col", axis=1, tiled=True),
        lax.all_gather(right_loc, "col", axis=1, tiled=True),
    )
    local_tiles = wavefunction.shape[0]
    tile_width = wavefunction.shape[3]
    mixed_rows = []
    for position in range(local_tiles):
        blocks = whole[left_src[0, position]]
        left_part = jnp.einsum(
            "kxy,ksyz->sxz", env_left[0, position], blocks, preferred_element_type=jnp.float32
        ).astype(jnp.bfloat16)
        mixed_rows.append(
            jnp.einsum(
                "ts,sxz->txz", two_site[0], left_part, preferred_element_type=jnp.float32
            ).astype(jnp.bfloat16)
        )
    mixed = jnp.stack(mixed_rows)
    col_iota = lax.broadcasted_iota(jnp.int32, (1, 1, tile_width), 2)
    received, recv_loc = (
        lax.all_to_all(mixed, "row", split_axis=1, concat_axis=0, tiled=True),
        lax.all_to_all(whole_loc, "row", split_axis=1, concat_axis=0, tiled=True),
    )
    pieces = []
    for column in range(received.shape[1]):
        chosen = env_right[0][recv_loc[:, column]]
        product = jnp.einsum(
            "axy,azy->axz", received[:, column], chosen, preferred_element_type=jnp.float32
        )
        col_limit = right_size[recv_loc[:, column]]
        inside = col_iota < col_limit[:, None, None]
        pieces.append(jnp.where(inside, product, 0.0).astype(jnp.bfloat16))
    term = lax.all_to_all(jnp.stack(pieces, axis=1), "row", split_axis=0, concat_axis=1, tiled=True)
    summed = lax.psum_scatter(
        term.astype(jnp.float32).astype(jnp.bfloat16), "col", scatter_dimension=1, tiled=True
    ).astype(jnp.float32)
    row_iota = lax.broadcasted_iota(jnp.int32, summed.shape, 2)
    inside_rows = row_iota < left_size[:, None, None, None]
    return jnp.where(inside_rows, summed, 0.0).astype(jnp.bfloat16)


def solution(mesh):
    placed = (
        P("row", "col", None, None),
        P("col", "row", None, None, None),
        P("col", "row", None),
        P("col", None, None),
        P("col", "row", None, None),
        P("row", "col"),
        P("row"),
        P("row"),
    )
    return jax.shard_map(
        per_device,
        mesh=mesh,
        in_specs=placed,
        out_specs=P("row", "col", None, None),
        check_vma=False,
    )
```

profile of v0, /device:TPU:1, one launch (start us, length us, event | category | flops | bytes accessed | tf_op | source)
XLA Modules:
  0.0 596.2 jit_solution(1501007717909477833)
XLA Ops:
  7.3 18.3 %all-gather = s32[16,1,4]{2,1,0:T(1,128)S(1)} all-gather(s32[1,1,4]{2,1,0:T(1,128)} %bitcast.158), channel_id=1, replica_groups=mesh['row'=8,'col'=16] {'col'}, dimensions={0}, use_global_device_ids=true | all-gather | bytes 272 | tf_op jit(solution)/shard_map/all_gather | solution.py:12
  26.3 9.6 %all-to-all-start = ((s32[4,8,2]{0,2,1:T(2,128)}), s32[4,8,2]{0,2,1:T(2,128)S(1)}, u32[]{:S(2)}, u32[]{:S(2)}) async-start(s32[4,8,2]{0,2,1:T(2,128)} %bitcast.3), calls=%async_computation | async-start | bytes 16384 | tf_op jit(solution)/shard_map/all_to_all | solution.py:31
  37.0 46.7 %all-gather.3.cloned.1.call-done = bf16[4,16,256,256]{3,2,1,0:T(8,128)(2,1)} async-done(((bf16[4,1,256,256]{3,2,1,0:T(8,128)(2,1)}), bf16[4,16,256,256]{3,2,1,0:T(8,128)(2,1)}) %all-gather.3.cloned.1.call-update) | async-done | bytes 8388624 | tf_op jit(solution)/shard_map/all_gather | solution.py:11
  83.7 6.0 fusion.62
  92.5 4.2 gather_fusion.7
  105.1 4.2 gather_fusion.2
  109.3 4.2 gather_fusion.3
  113.6 4.2 gather_fusion.8
  128.5 4.2 fusion.34
  144.0 4.9 fusion.31
  148.8 4.6 copy.38
  163.8 4.9 fusion.28
  180.6 4.9 fusion.37
  191.0 5.7 pad_maximum_fusion
  196.7 9.6 %copy.45 = bf16[4,16,256,256]{3,2,0,1:T(8,128)(2,1)} copy(bf16[4,16,256,256]{3,1,2,0:T(8,128)(2,1)} %pad_maximum_fusion) | data formatting | bytes 16777216 | tf_op jit(solution)/shard_map/stack | solution.py:27
  206.3 5.6 all-to-all-start.1
  220.9 85.0 %all-to-all-done.1 = bf16[4,16,256,256]{3,2,0,1:T(8,128)(2,1)} async-done(((bf16[4,16,256,256]{3,2,0,1:T(8,128)(2,1)}), bf16[4,16,256,256]{3,2,0,1:T(8,128)(2,1)}, u32[]{:S(2)}, u32[]{:S(2)}) %all-to-all-start.1) | async-done | bytes 8388640 | tf_op jit(solution)/shard_map/all_to_all | solution.py:30
  305.9 7.8 %copy.46 = bf16[4,8,2,256,256]{4,3,0,1,2:T(8,128)(2,1)} copy(bf16[4,8,2,256,256]{4,3,0,2,1:T(8,128)(2,1)} %bitcast.44) | data formatting | bytes 16777216 | tf_op jit(solution)/shard_map/all_to_all | solution.py:30
  313.6 5.8 fusion
  324.2 6.2 %pad_maximum_fusion.1 = bf16[32,2,256,256]{3,2,0,1:T(8,128)(2,1)} fusion(bf16[32,1,256,256]{3,2,0,1:T(8,128)(2,1)} %fusion.1, bf16[32,1,256,256]{3,2,0,1:T(8,128)(2,1)S(1)} %copy-done.9), kind=kLoop, calls=%fused_computation.11 | loop fusion | flops 4194304 | bytes 16777216 | tf_op jit(solution)/shard_map/stack | solution.py:42
  330.4 7.6 %copy.47 = bf16[32,2,256,256]{3,2,1,0:T(8,128)(2,1)} copy(bf16[32,2,256,256]{3,2,0,1:T(8,128)(2,1)} %pad_maximum_fusion.1) | data formatting | bytes 16777216 | tf_op jit(solution)/shard_map/stack | solution.py:42
  338.0 101.5 %all_to_all.55 = bf16[32,2,256,256]{3,2,1,0:T(8,128)(2,1)} all-to-all(bf16[32,2,256,256]{3,2,1,0:T(8,128)(2,1)} %copy.47), channel_id=1, replica_groups=mesh['row'=8,'col'=16] {'row'}, dimensions={0} | all-to-all | bytes 16777216 | tf_op jit(solution)/shard_map/all_to_all | solution.py:42
  439.5 7.6 %copy.48 = bf16[4,8,2,256,256]{4,3,2,1,0:T(8,128)(2,1)} copy(bf16[4,8,2,256,256]{4,3,2,0,1:T(8,128)(2,1)} %bitcast.153) | data formatting | bytes 16777216 | tf_op jit(solution)/shard_map/all_to_all | solution.py:42
  448.4 138.3 %all-reduce.3.cloned.1.call-done = bf16[4,16,256,256]{3,2,1,0:T(8,128)(2,1)} async-done(((bf16[4,16,256,256]{3,2,1,0:T(8,128)(2,1)}), bf16[4,16,256,256]{3,2,1,0:T(8,128)(2,1)}) %all-reduce.3.cloned.1.call-update) | async-done | bytes 8388624
  (75 shorter events, 81.2 us)
Async XLA Ops:
  6.5 206.2 %copy-start = (bf16[1,4,256,256]{3,2,1,0:T(8,128)(2,1)S(1)}, bf16[1,4,256,256]{3,2,1,0:T(8,128)(2,1)}, u32[]{:S(2)}) copy-start(bf16[1,4,256,256]{3,2,1,0:T(8,128)(2,1)} %param.12) | copy-start | bytes 1572868
  6.5 77.1 %all-gather.3.cloned.1.call-start = ((), (), s32[]{:S(2)}) async-start(), calls=%async_computation.3 | async-start | bytes 8912896 | tf_op jit(solution)/shard_map/all_gather | solution.py:11
  26.3 180.1 %all-to-all-start = ((s32[4,8,2]{0,2,1:T(2,128)}), s32[4,8,2]{0,2,1:T(2,128)S(1)}, u32[]{:S(2)}, u32[]{:S(2)}) async-start(s32[4,8,2]{0,2,1:T(2,128)} %bitcast.3), calls=%async_computation | async-start | bytes 16384 | tf_op jit(solution)/shard_map/all_to_all | solution.py:31
  124.4 4.1 copy-start.10
  148.8 4.6 copy-start.11
  153.4 2.1 copy-start.1
  155.5 6.0 copy-start.4
  174.1 4.1 copy-start.3
  188.8 1.6 copy-start.5
  188.8 2.2 copy-start.6
  206.3 5.6 copy-start.12
  206.3 99.5 %all-to-all-start.1 = ((bf16[4,16,256,256]{3,2,0,1:T(8,128)(2,1)}), bf16[4,16,256,256]{3,2,0,1:T(8,128)(2,1)}, u32[]{:S(2)}, u32[]{:S(2)}) async-start(bf16[4,16,256,256]{3,2,0,1:T(8,128)(2,1)} %copy.45), calls=%async_computation.1 | async-start | bytes 16777216 | tf_op jit(solution)/shard_map/all_to_all | solution.py:30
  212.0 374.7 %all-reduce.3.cloned.1.call-start = ((), (), s32[]{:S(2)}) async-start(), calls=%async_computation.4 | async-start | bytes 16777216
  305.8 7.8 %copy-start.8 = (bf16[32,256,256]{2,1,0:T(8,128)(2,1)S(1)}, bf16[32,256,256]{2,1,0:T(8,128)(2,1)}, u32[]{:S(2)}) copy-start(bf16[32,256,256]{2,1,0:T(8,128)(2,1)} %gather_fusion) | copy-start | bytes 12582916
  313.6 5.8 copy-start.2
  313.6 7.3 %copy-start.7 = (bf16[32,256,256]{2,1,0:T(8,128)(2,1)S(1)}, bf16[32,256,256]{2,1,0:T(8,128)(2,1)}, u32[]{:S(2)}) copy-start(bf16[32,256,256]{2,1,0:T(8,128)(2,1)} %gather_fusion.1) | copy-start | bytes 12582916
  321.0 3.3 copy-start.9
  447.1 0.7 copy-start.14
  447.1 139.6 %copy-start.13 = (s32[4]{0:T(128)S(1)}, s32[4]{0:T(128)}, u32[]{:S(2)}) copy-start(s32[4]{0:T(128)} %param.14) | copy-start | bytes 52
Sparse Core Ops, SparseCore 0:
  9.5 74.1 all-gather.2
  447.3 139.3 all-reduce.2
where the time goes:
time: 598 us; the launch traced here: 596 us
  waiting for transfers between devices  271 us (45%)
  local copies, waits for them, and re-layouts  125 us (21%)
  blocking collectives  120 us (20%)
  matrix products  34.7 us (6%)
  other arithmetic  17.2 us (3%)
  starting transfers between devices  15.2 us (3%)
  between operations  13.6 us (2%)
    unnamed x3, waiting for transfers between devices  139 us
    all_to_all x1, blocking collectives, per_device(): lax.all_to_all(jnp.stack(pieces, axis=1), 'row', split_axis=0, concat_axi...  101 us
    all_to_all x1, waiting for transfers between devices, per_device(): lax.all_to_all(mixed, 'row', split_axis=1, concat_axis=0, tiled=True)  85 us
    gather x17, local copies, waits for them, and re-layouts, per_device(): blocks = whole[left_src[0, position]]  65.5 us
    all_gather x1, waiting for transfers between devices, per_device(): lax.all_gather(wavefunction, 'col', axis=1, tiled=True)  46.7 us
    dot_general x4, matrix products, per_device(): jnp.einsum('kxy,ksyz->sxz', env_left[0, position], blocks, preferred_elem...  18.8 us
    all_gather x1, blocking collectives, per_device(): lax.all_gather(right_loc, 'col', axis=1, tiled=True)  18.3 us
    convert_element_type x4, local copies, waits for them, and re-layouts, per_device(): left_part = jnp.einsum('kxy,ksyz->sxz', env_left[0, position], blocks, pr...  14.6 us
  transfers between devices with their start and end apart: 4, of which 3 were waited for; matrix products, arithmetic and copies ran while one was open for 22% of the time, Pallas kernels for 0%

commit v1 on v0

--- a/solution.py
+++ b/solution.py
@@ -4,11 +4,32 @@
 from jax.sharding import PartitionSpec as P
 
 
+def collect(x, axis, dim):
+    size, here, extent = (lax.axis_size(axis), lax.axis_index(axis), x.shape[dim])
+    right = [(i, (i + 1) % size) for i in range(size)]
+    left = [(i, (i - 1) % size) for i in range(size)]
+    out = jnp.zeros((*x.shape[:dim], size * extent, *x.shape[dim + 1 :]), x.dtype)
+    out = lax.dynamic_update_slice_in_dim(out, x, here * extent, axis=dim)
+    from_left = from_right = x
+    middle = size // 2
+    for lap in range(1, middle + 1):
+        from_left = lax.ppermute(from_left, axis, right)
+        out = lax.dynamic_update_slice_in_dim(
+            out, from_left, (here - lap) % size * extent, axis=dim
+        )
+        if lap < size - middle:
+            from_right = lax.ppermute(from_right, axis, left)
+            out = lax.dynamic_update_slice_in_dim(
+                out, from_right, (here + lap) % size * extent, axis=dim
+            )
+    return out
+
+
 def per_device(
     wavefunction, env_left, left_src, two_site, env_right, right_loc, left_size, right_size
 ):
     whole, whole_loc = (
-        lax.all_gather(wavefunction, "col", axis=1, tiled=True),
+        collect(wavefunction, "col", 1),
         lax.all_gather(right_loc, "col", axis=1, tiled=True),
     )
     local_tiles = wavefunction.shape[0]

time: 598 us -> 672 us (1.12)
  starting transfers between devices: 15.2 us -> 53.5 us
  local copies, waits for them, and re-layouts: 125 us -> 149 us
  waiting for transfers between devices: 271 us -> 278 us
    ppermute x0 -> x15, waiting for transfers between devices: none -> 57.6 us  [the longest x8 38.7 us: collect(): from_left = lax.ppermute(from_left, axis, right)]
    all_gather x1 -> x0, waiting for transfers between devices: 46.7 us -> none  [per_device(): lax.all_gather(wavefunction, 'col', axis=1, tiled=True)]
    ppermute x0 -> x15, starting transfers between devices: none -> 33.2 us  [the longest x7 30.4 us: collect(): from_right = lax.ppermute(from_right, axis, left)]
    dynamic_update_slice x0 -> x16, local copies, waits for them, and re-layouts: none -> 19.4 us  [the longest x8 10.8 us: collect(): lax.dynamic_update_slice_in_dim(out, from_left, (here - lap) % size * ext...]
    unnamed x3 -> x2, waiting for transfers between devices: 139 us -> 135 us
  transfers between devices with their start and end apart: 4 -> 18, of which waited for: 3 -> 10; matrix products, arithmetic and copies ran while one was open for 22% -> 23% of each run, Pallas kernels for 0% -> 0%
where the time goes in v1:
time: 672 us; the launch traced here: 670 us
  waiting for transfers between devices  278 us (41%)
  local copies, waits for them, and re-layouts  149 us (22%)
  blocking collectives  124 us (18%)
  starting transfers between devices  53.5 us (8%)
  matrix products  34.6 us (5%)
  other arithmetic  17.2 us (3%)
  between operations  13.8 us (2%)
    unnamed x2, waiting for transfers between devices  135 us
    all_to_all x1, blocking collectives, per_device(): lax.all_to_all(jnp.stack(pieces, axis=1), 'row', split_axis=0, concat_axi...  101 us
    all_to_all x1, waiting for transfers between devices, per_device(): lax.all_to_all(mixed, 'row', split_axis=1, concat_axis=0, tiled=True)  85.1 us
    gather x17, local copies, waits for them, and re-layouts, per_device(): blocks = whole[left_src[0, position]]  65.7 us
    ppermute x8, waiting for transfers between devices, collect(): from_left = lax.ppermute(from_left, axis, right)  38.7 us
    ppermute x7, starting transfers between devices, collect(): from_right = lax.ppermute(from_right, axis, left)  30.4 us
    all_gather x1, blocking collectives, per_device(): lax.all_gather(right_loc, 'col', axis=1, tiled=True)  22.4 us
    ppermute x7, waiting for transfers between devices, collect(): from_right = lax.ppermute(from_right, axis, left)  18.9 us
  transfers between devices with their start and end apart: 18, of which 10 were waited for; matrix products, arithmetic and copies ran while one was open for 23% of the time, Pallas kernels for 0%

profile of v1, /device:TPU:1, one launch (start us, length us, event | category | flops | bytes accessed | tf_op | source)
XLA Modules:
  0.0 669.9 jit_solution(13849782225983410280)
XLA Ops:
  13.3 11.9 %collective-permute-done = bf16[4,1,256,256]{3,2,1,0:T(8,128)(2,1)S(1)} collective-permute-done((bf16[4,1,256,256]{3,2,1,0:T(8,128)(2,1)}, bf16[4,1,256,256]{3,2,1,0:T(8,128)(2,1)S(1)}, u32[]{:S(2)}, u32[]{:S(2)}) %collective-permute-start) | collective-permute-done | bytes 524320 | tf_op jit(solution)/shard_map/ppermute | solution.py:16
  30.0 10.7 %collective-permute-done.2 = bf16[4,1,256,256]{3,2,1,0:T(8,128)(2,1)S(1)} collective-permute-done((bf16[4,1,256,256]{3,2,1,0:T(8,128)(2,1)S(1)}, bf16[4,1,256,256]{3,2,1,0:T(8,128)(2,1)S(1)}, u32[]{:S(2)}, u32[]{:S(2)}) %collective-permute-start.2) | collective-permute-done | bytes 524320 | tf_op jit(solution)/shard_map/ppermute | solution.py:16
  45.5 9.8 %collective-permute-done.4 = bf16[4,1,256,256]{3,2,1,0:T(8,128)(2,1)S(1)} collective-permute-done((bf16[4,1,256,256]{3,2,1,0:T(8,128)(2,1)S(1)}, bf16[4,1,256,256]{3,2,1,0:T(8,128)(2,1)S(1)}, u32[]{:S(2)}, u32[]{:S(2)}) %collective-permute-start.4) | collective-permute-done | bytes 524320 | tf_op jit(solution)/shard_map/ppermute | solution.py:16
  55.3 22.4 %all-gather = s32[16,1,4]{2,1,0:T(1,128)S(1)} all-gather(s32[1,1,4]{2,1,0:T(1,128)} %bitcast.158), channel_id=1, replica_groups=mesh['row'=8,'col'=16] {'col'}, dimensions={0}, use_global_device_ids=true | all-gather | bytes 272 | tf_op jit(solution)/shard_map/all_gather | solution.py:33
  78.4 11.5 %all-to-all-start = ((s32[4,8,2]{0,2,1:T(2,128)}), s32[4,8,2]{0,2,1:T(2,128)S(1)}, u32[]{:S(2)}, u32[]{:S(2)}) async-start(s32[4,8,2]{0,2,1:T(2,128)} %bitcast.3), calls=%async_computation | async-start | bytes 16384 | tf_op jit(solution)/shard_map/all_to_all | solution.py:52
  97.7 7.0 %collective-permute-done.7 = bf16[4,1,256,256]{3,2,1,0:T(8,128)(2,1)} collective-permute-done((bf16[4,1,256,256]{3,2,1,0:T(8,128)(2,1)S(1)}, bf16[4,1,256,256]{3,2,1,0:T(8,128)(2,1)}, u32[]{:S(2)}, u32[]{:S(2)}) %collective-permute-start.7) | collective-permute-done | bytes 524320 | tf_op jit(solution)/shard_map/ppermute | solution.py:21
  112.8 6.9 %collective-permute-done.9 = bf16[4,1,256,256]{3,2,1,0:T(8,128)(2,1)} collective-permute-done((bf16[4,1,256,256]{3,2,1,0:T(8,128)(2,1)}, bf16[4,1,256,256]{3,2,1,0:T(8,128)(2,1)}, u32[]{:S(2)}, u32[]{:S(2)}) %collective-permute-start.9) | collective-permute-done | bytes 524320 | tf_op jit(solution)/shard_map/ppermute | solution.py:21
  119.7 5.5 collective-permute-start.11
  135.1 5.4 collective-permute-start.13
  149.9 6.3 collective-permute-done.14
  157.0 6.0 fusion.62
  237.4 4.9 fusion.34
  254.1 4.8 fusion.37
  264.5 5.7 pad_maximum_fusion
  270.3 9.7 %copy.45 = bf16[4,16,256,256]{3,2,0,1:T(8,128)(2,1)} copy(bf16[4,16,256,256]{3,1,2,0:T(8,128)(2,1)} %pad_maximum_fusion) | data formatting | bytes 16777216 | tf_op jit(solution)/shard_map/stack | solution.py:48
  280.0 8.8 %all-to-all-start.1 = ((bf16[4,16,256,256]{3,2,0,1:T(8,128)(2,1)}), bf16[4,16,256,256]{3,2,0,1:T(8,128)(2,1)}, u32[]{:S(2)}, u32[]{:S(2)}) async-start(bf16[4,16,256,256]{3,2,0,1:T(8,128)(2,1)} %copy.45), calls=%async_computation.1 | async-start | bytes 16777216 | tf_op jit(solution)/shard_map/all_to_all | solution.py:51
  297.5 85.1 %all-to-all-done.1 = bf16[4,16,256,256]{3,2,0,1:T(8,128)(2,1)} async-done(((bf16[4,16,256,256]{3,2,0,1:T(8,128)(2,1)}), bf16[4,16,256,256]{3,2,0,1:T(8,128)(2,1)}, u32[]{:S(2)}, u32[]{:S(2)}) %all-to-all-start.1) | async-done | bytes 8388640 | tf_op jit(solution)/shard_map/all_to_all | solution.py:51
  382.6 7.8 %copy.46 = bf16[4,8,2,256,256]{4,3,0,1,2:T(8,128)(2,1)} copy(bf16[4,8,2,256,256]{4,3,0,2,1:T(8,128)(2,1)} %bitcast.44) | data formatting | bytes 16777216 | tf_op jit(solution)/shard_map/all_to_all | solution.py:51
  390.4 5.8 fusion
  401.0 6.2 pad_maximum_fusion.1
  407.3 7.6 %copy.47 = bf16[32,2,256,256]{3,2,1,0:T(8,128)(2,1)} copy(bf16[32,2,256,256]{3,2,0,1:T(8,128)(2,1)} %pad_maximum_fusion.1) | data formatting | bytes 16777216 | tf_op jit(solution)/shard_map/stack | solution.py:63
  414.9 101.5 %all_to_all.55 = bf16[32,2,256,256]{3,2,1,0:T(8,128)(2,1)} all-to-all(bf16[32,2,256,256]{3,2,1,0:T(8,128)(2,1)} %copy.47), channel_id=1, replica_groups=mesh['row'=8,'col'=16] {'row'}, dimensions={0} | all-to-all | bytes 16777216 | tf_op jit(solution)/shard_map/all_to_all | solution.py:63
  516.3 7.7 %copy.48 = bf16[4,8,2,256,256]{4,3,2,1,0:T(8,128)(2,1)} copy(bf16[4,8,2,256,256]{4,3,2,0,1:T(8,128)(2,1)} %bitcast.153) | data formatting | bytes 16777216 | tf_op jit(solution)/shard_map/all_to_all | solution.py:63
  525.3 135.0 %all-reduce.3.cloned.1.call-done = bf16[4,16,256,256]{3,2,1,0:T(8,128)(2,1)} async-done(((bf16[4,16,256,256]{3,2,1,0:T(8,128)(2,1)}), bf16[4,16,256,256]{3,2,1,0:T(8,128)(2,1)}) %all-reduce.3.cloned.1.call-update) | async-done | bytes 8388624
  (123 shorter events, 162.1 us)
Async XLA Ops:
  6.5 282.9 %copy-start = (bf16[1,4,256,256]{3,2,1,0:T(8,128)(2,1)S(1)}, bf16[1,4,256,256]{3,2,1,0:T(8,128)(2,1)}, u32[]{:S(2)}) copy-start(bf16[1,4,256,256]{3,2,1,0:T(8,128)(2,1)} %param.12) | copy-start | bytes 1572868
  6.5 18.6 %collective-permute-start = (bf16[4,1,256,256]{3,2,1,0:T(8,128)(2,1)}, bf16[4,1,256,256]{3,2,1,0:T(8,128)(2,1)S(1)}, u32[]{:S(2)}, u32[]{:S(2)}) collective-permute-start(bf16[4,1,256,256]{3,2,1,0:T(8,128)(2,1)} %param.8), channel_id=1, source_target_pairs={{0,1},{1,2},{2,3},{3,4},{4,5},{5,6},{6,7},{7,8},{8,9},{9,10},{10,1... | collective-permute-start | bytes 1572872 | tf_op jit(solution)/shard_map/ppermute | solution.py:16
  8.6 16.6 %collective-permute-start.1 = (bf16[4,1,256,256]{3,2,1,0:T(8,128)(2,1)}, bf16[4,1,256,256]{3,2,1,0:T(8,128)(2,1)S(1)}, u32[]{:S(2)}, u32[]{:S(2)}) collective-permute-start(bf16[4,1,256,256]{3,2,1,0:T(8,128)(2,1)} %param.8), channel_id=1, source_target_pairs={{0,15},{1,0},{2,1},{3,2},{4,3},{5,4},{6,5},{7,6},{8,7},{9,8},{10,9... | collective-permute-start | bytes 1572872 | tf_op jit(solution)/shard_map/ppermute | solution.py:21
  25.2 15.5 %collective-permute-start.2 = (bf16[4,1,256,256]{3,2,1,0:T(8,128)(2,1)S(1)}, bf16[4,1,256,256]{3,2,1,0:T(8,128)(2,1)S(1)}, u32[]{:S(2)}, u32[]{:S(2)}) collective-permute-start(bf16[4,1,256,256]{3,2,1,0:T(8,128)(2,1)S(1)} %collective-permute-done), channel_id=1, source_target_pairs={{0,1},{1,2},{2,3},{3,4},{4,5},{5,6},{6,7},{7,8},{8,9},{9,10},{10,1... | collective-permute-start | bytes 1572872 | tf_op jit(solution)/shard_map/ppermute | solution.py:16
  25.2 15.5 %collective-permute-start.3 = (bf16[4,1,256,256]{3,2,1,0:T(8,128)(2,1)S(1)}, bf16[4,1,256,256]{3,2,1,0:T(8,128)(2,1)S(1)}, u32[]{:S(2)}, u32[]{:S(2)}) collective-permute-start(bf16[4,1,256,256]{3,2,1,0:T(8,128)(2,1)S(1)} %collective-permute-done.1), channel_id=1, source_target_pairs={{0,15},{1,0},{2,1},{3,2},{4,3},{5,4},{6,5},{7,6},{8,7},{9,8},{10,9... | collective-permute-start | bytes 1572872 | tf_op jit(solution)/shard_map/ppermute | solution.py:21
  40.7 14.6 %copy-start.12 = (bf16[4,1,256,256]{3,2,1,0:T(8,128)(2,1)}, bf16[4,1,256,256]{3,2,1,0:T(8,128)(2,1)S(1)}, u32[]{:S(2)}) copy-start(bf16[4,1,256,256]{3,2,1,0:T(8,128)(2,1)S(1)} %collective-permute-done.2) | copy-start | bytes 1572868
  40.7 14.6 %collective-permute-start.4 = (bf16[4,1,256,256]{3,2,1,0:T(8,128)(2,1)S(1)}, bf16[4,1,256,256]{3,2,1,0:T(8,128)(2,1)S(1)}, u32[]{:S(2)}, u32[]{:S(2)}) collective-permute-start(bf16[4,1,256,256]{3,2,1,0:T(8,128)(2,1)S(1)} %collective-permute-done.2), channel_id=1, source_target_pairs={{0,1},{1,2},{2,3},{3,4},{4,5},{5,6},{6,7},{7,8},{8,9},{9,10},{10,1... | collective-permute-start | bytes 1572872 | tf_op jit(solution)/shard_map/ppermute | solution.py:16
  40.7 50.3 %collective-permute-start.5 = (bf16[4,1,256,256]{3,2,1,0:T(8,128)(2,1)S(1)}, bf16[4,1,256,256]{3,2,1,0:T(8,128)(2,1)S(1)}, u32[]{:S(2)}, u32[]{:S(2)}) collective-permute-start(bf16[4,1,256,256]{3,2,1,0:T(8,128)(2,1)S(1)} %collective-permute-done.3), channel_id=1, source_target_pairs={{0,15},{1,0},{2,1},{3,2},{4,3},{5,4},{6,5},{7,6},{8,7},{9,8},{10,9... | collective-permute-start | bytes 1572872 | tf_op jit(solution)/shard_map/ppermute | solution.py:21
  55.3 36.7 %collective-permute-start.6 = (bf16[4,1,256,256]{3,2,1,0:T(8,128)(2,1)S(1)}, bf16[4,1,256,256]{3,2,1,0:T(8,128)(2,1)}, u32[]{:S(2)}, u32[]{:S(2)}) collective-permute-start(bf16[4,1,256,256]{3,2,1,0:T(8,128)(2,1)S(1)} %collective-permute-done.4), channel_id=1, source_target_pairs={{0,1},{1,2},{2,3},{3,4},{4,5},{5,6},{6,7},{7,8},{8,9},{9,10},{10,1... | collective-permute-start | bytes 1572872 | tf_op jit(solution)/shard_map/ppermute | solution.py:16
  78.4 201.6 %all-to-all-start = ((s32[4,8,2]{0,2,1:T(2,128)}), s32[4,8,2]{0,2,1:T(2,128)S(1)}, u32[]{:S(2)}, u32[]{:S(2)}) async-start(s32[4,8,2]{0,2,1:T(2,128)} %bitcast.3), calls=%async_computation | async-start | bytes 16384 | tf_op jit(solution)/shard_map/all_to_all | solution.py:52
  91.0 13.7 %collective-permute-start.7 = (bf16[4,1,256,256]{3,2,1,0:T(8,128)(2,1)S(1)}, bf16[4,1,256,256]{3,2,1,0:T(8,128)(2,1)}, u32[]{:S(2)}, u32[]{:S(2)}) collective-permute-start(bf16[4,1,256,256]{3,2,1,0:T(8,128)(2,1)S(1)} %collective-permute-done.5), channel_id=1, source_target_pairs={{0,15},{1,0},{2,1},{3,2},{4,3},{5,4},{6,5},{7,6},{8,7},{9,8},{10,9... | collective-permute-start | bytes 1572872 | tf_op jit(solution)/shard_map/ppermute | solution.py:21
  91.9 17.0 %collective-permute-start.8 = (bf16[4,1,256,256]{3,2,1,0:T(8,128)(2,1)}, bf16[4,1,256,256]{3,2,1,0:T(8,128)(2,1)}, u32[]{:S(2)}, u32[]{:S(2)}) collective-permute-start(bf16[4,1,256,256]{3,2,1,0:T(8,128)(2,1)} %collective-permute-done.6), channel_id=1, source_target_pairs={{0,1},{1,2},{2,3},{3,4},{4,5},{5,6},{6,7},{7,8},{8,9},{9,10},{10,1... | collective-permute-start | bytes 1572872 | tf_op jit(solution)/shard_map/ppermute | solution.py:16
  104.7 15.0 %collective-permute-start.9 = (bf16[4,1,256,256]{3,2,1,0:T(8,128)(2,1)}, bf16[4,1,256,256]{3,2,1,0:T(8,128)(2,1)}, u32[]{:S(2)}, u32[]{:S(2)}) collective-permute-start(bf16[4,1,256,256]{3,2,1,0:T(8,128)(2,1)} %collective-permute-done.7), channel_id=1, source_target_pairs={{0,15},{1,0},{2,1},{3,2},{4,3},{5,4},{6,5},{7,6},{8,7},{9,8},{10,9... | collective-permute-start | bytes 1572872 | tf_op jit(solution)/shard_map/ppermute | solution.py:21
  108.9 17.1 %collective-permute-start.10 = (bf16[4,1,256,256]{3,2,1,0:T(8,128)(2,1)}, bf16[4,1,256,256]{3,2,1,0:T(8,128)(2,1)}, u32[]{:S(2)}, u32[]{:S(2)}) collective-permute-start(bf16[4,1,256,256]{3,2,1,0:T(8,128)(2,1)} %collective-permute-done.8), channel_id=1, source_target_pairs={{0,1},{1,2},{2,3},{3,4},{4,5},{5,6},{6,7},{7,8},{8,9},{9,10},{10,1... | collective-permute-start | bytes 1572872 | tf_op jit(solution)/shard_map/ppermute | solution.py:16
  119.7 15.4 %collective-permute-start.11 = (bf16[4,1,256,256]{3,2,1,0:T(8,128)(2,1)}, bf16[4,1,256,256]{3,2,1,0:T(8,128)(2,1)S(1)}, u32[]{:S(2)}, u32[]{:S(2)}) collective-permute-start(bf16[4,1,256,256]{3,2,1,0:T(8,128)(2,1)} %collective-permute-done.9), channel_id=1, source_target_pairs={{0,15},{1,0},{2,1},{3,2},{4,3},{5,4},{6,5},{7,6},{8,7},{9,8},{10,9... | collective-permute-start | bytes 1572872 | tf_op jit(solution)/shard_map/ppermute | solution.py:21
  126.0 16.3 %collective-permute-start.12 = (bf16[4,1,256,256]{3,2,1,0:T(8,128)(2,1)}, bf16[4,1,256,256]{3,2,1,0:T(8,128)(2,1)S(1)}, u32[]{:S(2)}, u32[]{:S(2)}) collective-permute-start(bf16[4,1,256,256]{3,2,1,0:T(8,128)(2,1)} %collective-permute-done.10), channel_id=1, source_target_pairs={{0,1},{1,2},{2,3},{3,4},{4,5},{5,6},{6,7},{7,8},{8,9},{9,10},{10,1... | collective-permute-start | bytes 1572872 | tf_op jit(solution)/shard_map/ppermute | solution.py:16
  135.1 14.0 %collective-permute-start.13 = (bf16[4,1,256,256]{3,2,1,0:T(8,128)(2,1)S(1)}, bf16[4,1,256,256]{3,2,1,0:T(8,128)(2,1)S(1)}, u32[]{:S(2)}, u32[]{:S(2)}) collective-permute-start(bf16[4,1,256,256]{3,2,1,0:T(8,128)(2,1)S(1)} %collective-permute-done.11), channel_id=1, source_target_pairs={{0,15},{1,0},{2,1},{3,2},{4,3},{5,4},{6,5},{7,6},{8,7},{9,8},{10,9... | collective-permute-start | bytes 1572872 | tf_op jit(solution)/shard_map/ppermute | solution.py:21
  142.4 13.9 %collective-permute-start.14 = (bf16[4,1,256,256]{3,2,1,0:T(8,128)(2,1)S(1)}, bf16[4,1,256,256]{3,2,1,0:T(8,128)(2,1)S(1)}, u32[]{:S(2)}, u32[]{:S(2)}) collective-permute-start(bf16[4,1,256,256]{3,2,1,0:T(8,128)(2,1)S(1)} %collective-permute-done.12), channel_id=1, source_target_pairs={{0,1},{1,2},{2,3},{3,4},{4,5},{5,6},{6,7},{7,8},{8,9},{9,10},{10,1... | collective-permute-start | bytes 1572872 | tf_op jit(solution)/shard_map/ppermute | solution.py:16
  279.9 8.8 %copy-start.14 = (s32[4]{0:T(128)S(1)}, s32[4]{0:T(128)}, u32[]{:S(2)}) copy-start(s32[4]{0:T(128)} %param.15) | copy-start | bytes 52
  280.0 102.7 %all-to-all-start.1 = ((bf16[4,16,256,256]{3,2,0,1:T(8,128)(2,1)}), bf16[4,16,256,256]{3,2,0,1:T(8,128)(2,1)}, u32[]{:S(2)}, u32[]{:S(2)}) async-start(bf16[4,16,256,256]{3,2,0,1:T(8,128)(2,1)} %copy.45), calls=%async_computation.1 | async-start | bytes 16777216 | tf_op jit(solution)/shard_map/all_to_all | solution.py:51
  288.8 371.5 %all-reduce.3.cloned.1.call-start = ((), (), s32[]{:S(2)}) async-start(), calls=%async_computation.3 | async-start | bytes 16777216
  382.6 7.8 %copy-start.8 = (bf16[32,256,256]{2,1,0:T(8,128)(2,1)S(1)}, bf16[32,256,256]{2,1,0:T(8,128)(2,1)}, u32[]{:S(2)}) copy-start(bf16[32,256,256]{2,1,0:T(8,128)(2,1)} %gather_fusion) | copy-start | bytes 12582916
  390.4 7.3 %copy-start.7 = (bf16[32,256,256]{2,1,0:T(8,128)(2,1)S(1)}, bf16[32,256,256]{2,1,0:T(8,128)(2,1)}, u32[]{:S(2)}) copy-start(bf16[32,256,256]{2,1,0:T(8,128)(2,1)} %gather_fusion.1) | copy-start | bytes 12582916
  524.0 136.3 %copy-start.15 = (s32[4]{0:T(128)S(1)}, s32[4]{0:T(128)}, u32[]{:S(2)}) copy-start(s32[4]{0:T(128)} %param.14) | copy-start | bytes 52
  (11 other events, 38.7 us)
Sparse Core Ops, SparseCore 0:
  524.1 136.0 all-reduce.2
